TPU v7x, 512 devices: a whole 4x8x8 slice. The times are simulated.
512 devices in a mesh: ctx: 128 (over x, z, y_lo), chan: 4 (over y_hi, core).
Axes of the slice: x: 4, y: 8 (y_hi: 2, y_lo: 4; y = y_hi * 4 + y_lo), z: 8, core: 2. Of those that a mesh axis runs over, the one named last changes fastest.
Arguments:
- signal: bfloat16 [128, 131072], P('chan', 'ctx'), may hold values from -6 to 6
- gating: bfloat16 [128, 131072], P('chan', 'ctx'), may hold values from -6 to 6
- cotangent: bfloat16 [128, 131072], P('chan', 'ctx'), may hold values from -6 to 6
- filters: float32 [32, 131072], P(None, 'ctx'), may hold values from -1 to 1
- skip_weight: float32 [128], P('chan'), may hold values from 0.5 to 1.5
Outputs:
- grad_signal: bfloat16 [128, 131072], P('chan', 'ctx')
- grad_gating: bfloat16 [128, 131072], P('chan', 'ctx')
- grad_filters: float32 [32, 131072], P('chan', 'ctx')
All inputs are finite; a program needn't handle non-finite values.
Results may differ from a plain program's by a relative error of at most 0.0075.
Values may be sent and summed in bfloat16 or wider, within the bound.
A program may use at most 64 MiB of HBM per device.

v0:
```python
import math

import jax
import jax.numpy as jnp
import numpy as np
from jax import lax
from jax.experimental import pallas as pl
from jax.experimental.pallas import tpu as pltpu
from jax.sharding import PartitionSpec as P

MESH = pl.DeviceIdType.MESH
F32 = jnp.float32
BF16 = jnp.bfloat16
COARSE = 512
FINE = 256
TILE = 256


def tables(total):
    shift = 0.25
    coarse = np.arange(COARSE) - shift
    angle = 2.0 * np.pi * ((coarse[:, None] * coarse[None, :]) / COARSE)
    big = np.concatenate([np.cos(angle), -np.sin(angle)], axis=1)
    fine = np.arange(FINE)
    angle = 2.0 * np.pi * ((coarse[:, None] * fine[None, :]) / total + coarse[:, None] * shift / COARSE)
    turn = np.concatenate([np.cos(angle), -np.sin(angle)], axis=1)
    angle = 2.0 * np.pi * ((fine[:, None] * fine[None, :]) % FINE) / FINE
    cosine, sine = np.cos(angle), np.sin(angle)
    ahead = np.block([[cosine, -sine], [sine, cosine]])
    back = np.block([[cosine, sine], [-sine, cosine]])
    as_bf16 = lambda table: jnp.asarray(table.astype(np.float32)).astype(BF16)
    return (as_bf16(big), jnp.asarray(turn.astype(np.float32)), as_bf16(ahead), as_bf16(back))


def dot(left, right):
    return jnp.dot(left, right, preferred_element_type=F32)


def kernel(
    signal, gating, cotangent, filters, big_hbm, turn_hbm, ahead_hbm, back_hbm,
    conv_out, back_out, corr_out,
    send, got, stage, big, turn, ahead, back, block, spec, mixed, leave, conv_in, back_in, corr_in,
    table_sem, own_sem, send_sem, got_sem, leave_sem, land_sem,
):
    place = lax.axis_index("ctx")
    chan = lax.axis_index("chan")
    rows = 32
    peers = 128
    lane = 128
    total = COARSE * FINE
    worker_low = 1 + chan % 2
    column = place // 4
    is_worker = place % 4 == worker_low
    home = column // 8
    foreign = home != chan

    table_copies = [
        pltpu.make_async_copy(big_hbm, big, table_sem.at[0]),
        pltpu.make_async_copy(turn_hbm, turn, table_sem.at[1]),
        pltpu.make_async_copy(ahead_hbm, ahead, table_sem.at[2]),
        pltpu.make_async_copy(back_hbm, back, table_sem.at[3]),
    ]

    barrier = pltpu.get_barrier_semaphore()

    def greet(ctx, other):
        pl.semaphore_signal(barrier, inc=1, device_id=(ctx, other), device_id_type=MESH)

    @pl.when(is_worker)
    def _():
        for copy in table_copies:
            copy.start()

        @pl.loop(1, peers)
        def _(step):
            greet((place + step) % peers, chan)

    @pl.loop(0, 8)
    def _(step):
        filt = 8 * chan + step
        for hop in range(1, 4):
            other = (chan + hop) % 4
            greet(4 * filt + 1 + other % 2, other)

    def spread(values, kind):
        for piece in range(8):
            stage[pl.ds(piece, rows, stride=8), :] = values[:, piece * lane : (piece + 1) * lane]
        send[:, kind] = stage[0 : rows * 8, :].reshape(rows, 8, lane).astype(BF16)

    spread(signal[...].astype(F32), 0)
    spread(filters[...], 1)
    gated = (cotangent[...].astype(F32) * gating[...].astype(F32)).astype(BF16)
    spread(gated.astype(F32), 2)

    @pl.when(is_worker)
    def _():
        @pl.when(foreign)
        def _():
            pl.semaphore_wait(barrier, 31 + peers)

        @pl.when(jnp.logical_not(foreign))
        def _():
            pl.semaphore_wait(barrier, 31)

    @pl.when(jnp.logical_not(is_worker))
    def _():
        pl.semaphore_wait(barrier, 32)

    parts = ((0, 2), (2, 3))
    for index, (low, high) in enumerate(parts):

        @pl.loop(0, rows)
        def _(step):
            filt = (column + step) % rows
            target = 4 * filt + worker_low

            @pl.when(target != place)
            def _():
                pltpu.make_async_remote_copy(
                    send.at[filt, low:high], got.at[place, low:high],
                    send_sem.at[index], got_sem.at[index],
                    device_id=(target, chan), device_id_type=MESH,
                ).start()

    def drain(ref, sem):
        pltpu.make_async_copy(ref, ref, sem).wait()

    def ahead_transform(kind):
        stage[...] = got[:, kind].astype(F32).reshape(peers * 8, lane)
        for half in range(2):
            block[:, half * lane : (half + 1) * lane] = stage[pl.ds(half, COARSE, stride=2), :].astype(BF16)

        @pl.loop(0, COARSE // TILE)
        def _(step):
            at = pl.ds(pl.multiple_of(step * TILE, TILE), TILE)
            real = dot(big[at, 0:COARSE], block[...])
            imag = dot(big[at, COARSE:], block[...])
            cosine = turn[at, 0:FINE]
            sine = turn[at, FINE:]
            turned = jnp.concatenate(
                [real * cosine - imag * sine, real * sine + imag * cosine], axis=1
            ).astype(BF16)
            spec[kind, at, :] = dot(turned, ahead[...])

    def back_transform(left, right, conjugate, kind):
        @pl.loop(0, COARSE // TILE)
        def _(step):
            at = pl.ds(pl.multiple_of(step * TILE, TILE), TILE)
            left_real = spec[left, at, 0:FINE]
            left_imag = spec[left, at, FINE:]
            right_real = spec[right, at, 0:FINE]
            right_imag = spec[right, at, FINE:]
            if conjugate:
                real = left_real * right_real + left_imag * right_imag
                imag = left_real * right_imag - left_imag * right_real
            else:
                real = left_real * right_real - left_imag * right_imag
                imag = left_real * right_imag + left_imag * right_real
            joined = jnp.concatenate([real, imag], axis=1).astype(BF16)
            half = dot(joined, back[...])
            real, imag = half[:, 0:FINE], half[:, FINE:]
            cosine = turn[at, 0:FINE]
            sine = turn[at, FINE:]
            mixed[at, :] = (real * cosine + imag * sine).astype(BF16)
            low = pl.ds(pl.multiple_of(COARSE + step * TILE, TILE), TILE)
            mixed[low, :] = (imag * cosine - real * sine).astype(BF16)

        @pl.loop(0, COARSE // TILE)
        def _(step):
            at = pl.ds(pl.multiple_of(step * TILE, TILE), TILE)
            time = dot(big[at, :], mixed[...]) * (1.0 / total)
            for part in range(2):
                stage[pl.ds(2 * step * TILE + part, TILE, stride=2), :] = time[
                    :, part * lane : (part + 1) * lane
                ]

        leave[kind] = stage[...].reshape(peers, 8, lane).astype(BF16)

    def scatter(kind, landing):
        @pl.loop(1, peers)
        def _(step):
            target = (place + step) % peers
            pltpu.make_async_remote_copy(
                leave.at[kind, target], landing.at[column],
                leave_sem.at[kind], land_sem.at[kind],
                device_id=(target, chan), device_id_type=MESH,
            ).start()

        pltpu.make_async_copy(leave.at[kind, place], landing.at[column], own_sem.at[1 + kind]).start()

    @pl.when(is_worker)
    def _():
        pltpu.make_async_copy(send.at[column], got.at[place], own_sem.at[0]).start()
        for copy in table_copies:
            copy.wait()
        pltpu.make_async_copy(send.at[column], got.at[place], own_sem.at[0]).wait()
        drain(got.at[0 : peers - 1, 0:2], got_sem.at[0])
        ahead_transform(0)
        ahead_transform(1)
        back_transform(0, 1, False, 0)
        scatter(0, conv_in)
        drain(got.at[0 : peers - 1, 2:3], got_sem.at[1])
        ahead_transform(2)
        back_transform(1, 2, True, 1)
        scatter(1, back_in)
        back_transform(0, 2, True, 2)

        @pl.loop(0, peers)
        def _(step):
            target = (place + step) % peers

            @pl.when(jnp.logical_or(foreign, step > 0))
            def _():
                pltpu.make_async_remote_copy(
                    leave.at[2, target], corr_in.at[column % 8, chan],
                    leave_sem.at[2], land_sem.at[2],
                    device_id=(target, home), device_id_type=MESH,
                ).start()

        @pl.when(jnp.logical_not(foreign))
        def _():
            pltpu.make_async_copy(leave.at[2, place], corr_in.at[column % 8, chan], own_sem.at[3]).start()

        drain(send.at[0 : rows - 1, 0:2], send_sem.at[0])
        drain(send.at[0 : rows - 1, 2:3], send_sem.at[1])
        for kind, landing in ((0, conv_in), (1, back_in)):
            pltpu.make_async_copy(leave.at[kind, place], landing.at[column], own_sem.at[1 + kind]).wait()
            drain(landing.at[0 : rows - 1], land_sem.at[kind])

        @pl.when(foreign)
        def _():
            drain(corr_in, land_sem.at[2])

        @pl.when(jnp.logical_not(foreign))
        def _():
            pltpu.make_async_copy(leave.at[2, place], corr_in.at[column % 8, chan], own_sem.at[3]).wait()
            drain(leave.at[2, 0 : rows - 1], land_sem.at[2])

    @pl.when(jnp.logical_not(is_worker))
    def _():
        drain(send.at[0:rows, 0:2], send_sem.at[0])
        drain(send.at[0:rows, 2:3], send_sem.at[1])
        drain(conv_in, land_sem.at[0])
        drain(back_in, land_sem.at[1])
        drain(corr_in, land_sem.at[2])

    def gather(values, count, result):
        stage[0 : count * 8, :] = values.reshape(count * 8, lane)
        for piece in range(8):
            result[:, piece * lane : (piece + 1) * lane] = stage[pl.ds(piece, count, stride=8), :].astype(
                result.dtype
            )

    gather(conv_in[...].astype(F32), rows, conv_out)
    gather(back_in[...].astype(F32), rows, back_out)
    gather(jnp.sum(corr_in[...].astype(F32), axis=1), 8, corr_out)

    @pl.when(is_worker)
    def _():
        drain(leave.at[0, 0 : peers - 1], leave_sem.at[0])
        drain(leave.at[1, 0 : peers - 1], leave_sem.at[1])

        @pl.when(foreign)
        def _():
            drain(leave.at[2], leave_sem.at[2])

        @pl.when(jnp.logical_not(foreign))
        def _():
            drain(leave.at[2, 0 : peers - 1], leave_sem.at[2])


def exchange(signal, gating, cotangent, filters):
    rows, length = signal.shape
    total = COARSE * FINE
    peers = total // length
    table_list = tables(total)
    vmem = pl.BlockSpec(memory_space=pltpu.VMEM)
    hbm = pl.BlockSpec(memory_space=pl.ANY)
    return pl.pallas_call(
        kernel,
        out_shape=(
            jax.ShapeDtypeStruct((rows, length), F32),
            jax.ShapeDtypeStruct((rows, length), F32),
            jax.ShapeDtypeStruct((8, length), F32),
        ),
        in_specs=[vmem] * 4 + [hbm] * 4,
        out_specs=(vmem, vmem, vmem),
        scratch_shapes=[
            pltpu.VMEM((rows, 3, 8, 128), BF16),
            pltpu.VMEM((peers, 3, 8, 128), BF16),
            pltpu.VMEM((peers * 8, 128), F32),
            pltpu.VMEM((COARSE, 2 * COARSE), BF16),
            pltpu.VMEM((COARSE, 2 * FINE), F32),
            pltpu.VMEM((2 * FINE, 2 * FINE), BF16),
            pltpu.VMEM((2 * FINE, 2 * FINE), BF16),
            pltpu.VMEM((COARSE, FINE), BF16),
            pltpu.VMEM((3, COARSE, 2 * FINE), F32),
            pltpu.VMEM((2 * COARSE, FINE), BF16),
            pltpu.VMEM((3, peers, 8, 128), BF16),
            pltpu.VMEM((rows, 8, 128), BF16),
            pltpu.VMEM((rows, 8, 128), BF16),
            pltpu.VMEM((8, 4, 8, 128), BF16),
            pltpu.SemaphoreType.DMA((4,)),
            pltpu.SemaphoreType.DMA((4,)),
            pltpu.SemaphoreType.DMA((2,)),
            pltpu.SemaphoreType.DMA((2,)),
            pltpu.SemaphoreType.DMA((3,)),
            pltpu.SemaphoreType.DMA((3,)),
        ],
        compiler_params=pltpu.CompilerParams(
            collective_id=0, has_side_effects=True, vmem_limit_bytes=40 * 1024 * 1024
        ),
        name="exchange",
    )(signal, gating, cotangent, filters, *table_list)


def per_device(signal, gating, cotangent, filters, skip_weight):
    rows, length = signal.shape
    conv, back, corr = exchange(signal, gating, cotangent, filters)
    weight = skip_weight[:, None]
    cot = cotangent.astype(F32)
    gated = (cot * gating.astype(F32)).astype(BF16).astype(F32)
    grad_gating = (cot * (conv + weight * signal.astype(F32))).astype(BF16)
    grad_signal = (back + weight * gated).astype(BF16)
    group = lax.axis_size("chan") * rows // filters.shape[0]
    grad_filters = corr * (1.0 / math.sqrt(COARSE * FINE * group))
    return (grad_signal, grad_gating, grad_filters)


def solution(mesh):
    in_specs = (P("chan", "ctx"), P("chan", "ctx"), P("chan", "ctx"), P(None, "ctx"), P("chan"))
    out_specs = (P("chan", "ctx"), P("chan", "ctx"), P("chan", "ctx"))
    return jax.shard_map(
        per_device, mesh=mesh, in_specs=in_specs, out_specs=out_specs, check_vma=False
    )
```

profile of v0, /device:TPU:1, one launch (start us, length us, event | category | flops | bytes accessed | tf_op | source)
XLA Modules:
  0.0 61.6 jit_solution(1876058375592613347)
XLA Ops:
  0.6 0.0 copy-start
  0.6 1.2 %copy-done = bf16[512,1024]{1,0:T(8,128)(2,1)S(1)} copy-done((bf16[512,1024]{1,0:T(8,128)(2,1)S(1)}, bf16[512,1024]{1,0:T(8,128)(2,1)}, u32[]{:S(2)}) %copy-start) | copy-done | bytes 1048600
  1.9 0.0 copy-start.1
  1.9 1.2 %copy-done.1 = f32[512,512]{1,0:T(8,128)S(1)} copy-done((f32[512,512]{1,0:T(8,128)S(1)}, f32[512,512]{1,0:T(8,128)}, u32[]{:S(2)}) %copy-start.1) | copy-done | bytes 1048600
  3.1 0.0 copy-start.2
  3.1 1.0 %copy-done.2 = bf16[512,512]{1,0:T(8,128)(2,1)S(1)} copy-done((bf16[512,512]{1,0:T(8,128)(2,1)S(1)}, bf16[512,512]{1,0:T(8,128)(2,1)}, u32[]{:S(2)}) %copy-start.2) | copy-done | bytes 524312
  4.1 0.0 copy-start.3
  4.1 1.0 %copy-done.3 = bf16[512,512]{1,0:T(8,128)(2,1)S(1)} copy-done((bf16[512,512]{1,0:T(8,128)(2,1)S(1)}, bf16[512,512]{1,0:T(8,128)(2,1)}, u32[]{:S(2)}) %copy-start.3) | copy-done | bytes 524312
  5.2 0.0 copy-start.4
  5.2 0.8 %copy-done.4 = bf16[32,1024]{1,0:T(8,128)(2,1)S(1)} copy-done((bf16[32,1024]{1,0:T(8,128)(2,1)S(1)}, bf16[32,1024]{1,0:T(8,128)(2,1)}, u32[]{:S(2)}) %copy-start.4) | copy-done | bytes 65560
  6.0 0.0 copy-start.5
  6.0 0.8 %copy-done.5 = bf16[32,1024]{1,0:T(8,128)(2,1)S(1)} copy-done((bf16[32,1024]{1,0:T(8,128)(2,1)S(1)}, bf16[32,1024]{1,0:T(8,128)(2,1)}, u32[]{:S(2)}) %copy-start.5) | copy-done | bytes 65560
  6.8 0.0 copy-start.6
  6.9 0.8 %copy-done.6 = bf16[32,1024]{1,0:T(8,128)(2,1)S(1)} copy-done((bf16[32,1024]{1,0:T(8,128)(2,1)S(1)}, bf16[32,1024]{1,0:T(8,128)(2,1)}, u32[]{:S(2)}) %copy-start.6) | copy-done | bytes 65560
  7.7 0.0 copy-start.7
  7.7 0.9 %copy-done.7 = f32[32,1024]{1,0:T(8,128)S(1)} copy-done((f32[32,1024]{1,0:T(8,128)S(1)}, f32[32,1024]{1,0:T(8,128)}, u32[]{:S(2)}) %copy-start.7) | copy-done | bytes 131096
  8.6 51.0 %exchange.1 = (f32[32,1024]{1,0:T(8,128)S(1)}, f32[32,1024]{1,0:T(8,128)S(1)}, f32[8,1024]{1,0:T(8,128)S(1)}) custom-call(bf16[32,1024]{1,0:T(8,128)(2,1)S(1)} %copy-done.5, bf16[32,1024]{1,0:T(8,128)(2,1)S(1)} %copy-done.6, bf16[32,1024]{1,0:T(8,128)(2,1)S(1)} %copy-done.4, f32[32,1024]{1,0:T(8,128)S(1)} %copy-done.7, bf16[512,1024]{1,0:T(8,128)(2,1)S(1)} %copy-done, ...), custom_call_target="tpu_custom_call" | custom-call | tf_op jit(solution)/shard_map/exchange/pallas_call | solution.py:279
  59.6 0.0 copy-start.8
  59.6 0.6 %copy-done.8 = f32[32]{0:T(128)S(1)} copy-done((f32[32]{0:T(128)S(1)}, f32[32]{0:T(128)}, u32[]{:S(2)}) %copy-start.8) | copy-done | bytes 152
  60.2 0.8 %fusion.1 = (bf16[32,1024]{1,0:T(8,128)(2,1)}, bf16[32,1024]{1,0:T(8,128)(2,1)}) fusion(bf16[32,1024]{1,0:T(8,128)(2,1)S(1)} %copy-done.4, f32[32,1024]{1,0:T(8,128)S(1)} %get-tuple-element.7, bf16[32,1024]{1,0:T(8,128)(2,1)S(1)} %copy-done.5, f32[32]{0:T(128)S(1)} %copy-done.8, f32[32,1024]{1,0:T(8,128)S(1)} %get-tuple-element.6, ...), kind=kLoop, calls=%fused_computation.3 | loop fusion | flops 425984 | bytes 589952 | tf_op jit(solution)/shard_map/convert_element_type | solution.py:323
  61.0 0.6 %broadcast_multiply_fusion = f32[8,1024]{1,0:T(8,128)} fusion(f32[8,1024]{1,0:T(8,128)S(1)} %get-tuple-element.8), kind=kLoop, calls=%fused_computation.5 | loop fusion | flops 8192 | bytes 65536 | tf_op jit(solution)/shard_map/mul | solution.py:326
Async XLA Ops:
  0.6 1.2 %copy-start = (bf16[512,1024]{1,0:T(8,128)(2,1)S(1)}, bf16[512,1024]{1,0:T(8,128)(2,1)}, u32[]{:S(2)}) copy-start(bf16[512,1024]{1,0:T(8,128)(2,1)} %constant.14.big_hbm) | copy-start | bytes 3145732
  1.9 1.2 %copy-start.1 = (f32[512,512]{1,0:T(8,128)S(1)}, f32[512,512]{1,0:T(8,128)}, u32[]{:S(2)}) copy-start(f32[512,512]{1,0:T(8,128)} %constant.11.clone.turn_hbm) | copy-start | bytes 3145732
  3.1 1.0 %copy-start.2 = (bf16[512,512]{1,0:T(8,128)(2,1)S(1)}, bf16[512,512]{1,0:T(8,128)(2,1)}, u32[]{:S(2)}) copy-start(bf16[512,512]{1,0:T(8,128)(2,1)} %constant.16.back_hbm) | copy-start | bytes 1572868
  4.1 1.0 %copy-start.3 = (bf16[512,512]{1,0:T(8,128)(2,1)S(1)}, bf16[512,512]{1,0:T(8,128)(2,1)}, u32[]{:S(2)}) copy-start(bf16[512,512]{1,0:T(8,128)(2,1)} %constant.15.ahead_hbm) | copy-start | bytes 1572868
  5.2 0.8 %copy-start.4 = (bf16[32,1024]{1,0:T(8,128)(2,1)S(1)}, bf16[32,1024]{1,0:T(8,128)(2,1)}, u32[]{:S(2)}) copy-start(bf16[32,1024]{1,0:T(8,128)(2,1)} %cotangent.1) | copy-start | bytes 196612
  6.0 0.8 %copy-start.5 = (bf16[32,1024]{1,0:T(8,128)(2,1)S(1)}, bf16[32,1024]{1,0:T(8,128)(2,1)}, u32[]{:S(2)}) copy-start(bf16[32,1024]{1,0:T(8,128)(2,1)} %signal.1) | copy-start | bytes 196612
  6.8 0.8 %copy-start.6 = (bf16[32,1024]{1,0:T(8,128)(2,1)S(1)}, bf16[32,1024]{1,0:T(8,128)(2,1)}, u32[]{:S(2)}) copy-start(bf16[32,1024]{1,0:T(8,128)(2,1)} %gating.1) | copy-start | bytes 196612
  7.7 0.9 %copy-start.7 = (f32[32,1024]{1,0:T(8,128)S(1)}, f32[32,1024]{1,0:T(8,128)}, u32[]{:S(2)}) copy-start(f32[32,1024]{1,0:T(8,128)} %filters.1) | copy-start | bytes 393220
  59.6 0.7 %copy-start.8 = (f32[32]{0:T(128)S(1)}, f32[32]{0:T(128)}, u32[]{:S(2)}) copy-start(f32[32]{0:T(128)} %param.13) | copy-start | bytes 388
where the time goes:
time: 62.1 us; the launch traced here: 61.6 us
  Pallas kernels  51 us (82%)
  local copies, waits for them, and re-layouts  8.6 us (14%)
  other arithmetic  1.37 us (2%)
  between operations  0.66 us (1%)
    pallas_call x1, Pallas kernels, exchange(): pl.pallas_call(kernel, out_shape=(jax.ShapeDtypeStruct((rows, length), F3...  51 us
    unnamed x18, local copies, waits for them, and re-layouts  8.6 us

commit v1 on v0

--- a/solution.py
+++ b/solution.py
@@ -37,10 +37,10 @@
 
 
 def kernel(
-    signal, gating, cotangent, filters, big_hbm, turn_hbm, ahead_hbm, back_hbm,
+    signal_hbm, gating_hbm, cotangent_hbm, filters_hbm, weight_hbm, big_hbm, turn_hbm, ahead_hbm, back_hbm,
     conv_out, back_out, corr_out,
-    send, got, stage, big, turn, ahead, back, block, spec, mixed, leave, conv_in, back_in, corr_in,
-    table_sem, own_sem, send_sem, got_sem, leave_sem, land_sem,
+    signal, gating, cotangent, filters, weight, direct_signal, direct_gated, send, got, stage, big, turn, ahead, back, block, spec, mixed, leave, conv_in, back_in, corr_in,
+    load_sem, table_sem, own_sem, send_sem, got_sem, leave_sem, land_sem,
 ):
     place = lax.axis_index("ctx")
     chan = lax.axis_index("chan")
@@ -54,6 +54,20 @@
     home = column // 8
     foreign = home != chan
 
+    load_copies = [
+        pltpu.make_async_copy(source, target, load_sem.at[index])
+        for index, (source, target) in enumerate(
+            (
+                (signal_hbm, signal),
+                (filters_hbm, filters),
+                (cotangent_hbm, cotangent),
+                (gating_hbm, gating),
+                (weight_hbm, weight),
+            )
+        )
+    ]
+    for copy in load_copies:
+        copy.start()
     table_copies = [
         pltpu.make_async_copy(big_hbm, big, table_sem.at[0]),
         pltpu.make_async_copy(turn_hbm, turn, table_sem.at[1]),
@@ -87,10 +101,22 @@
             stage[pl.ds(piece, rows, stride=8), :] = values[:, piece * lane : (piece + 1) * lane]
         send[:, kind] = stage[0 : rows * 8, :].reshape(rows, 8, lane).astype(BF16)
 
+    load_copies[0].wait()
     spread(signal[...].astype(F32), 0)
+    load_copies[1].wait()
     spread(filters[...], 1)
+    load_copies[2].wait()
+    load_copies[3].wait()
     gated = (cotangent[...].astype(F32) * gating[...].astype(F32)).astype(BF16)
     spread(gated.astype(F32), 2)
+    load_copies[4].wait()
+    across = weight[...].reshape(1, rows) * jnp.ones((rows, 1), F32)
+    diagonal = lax.broadcasted_iota(jnp.int32, (rows, rows), 0) == lax.broadcasted_iota(
+        jnp.int32, (rows, rows), 1
+    )
+    down = jnp.sum(jnp.where(diagonal, across, 0.0), axis=1, keepdims=True)
+    direct_signal[...] = down * signal[...].astype(F32)
+    direct_gated[...] = down * gated.astype(F32)
 
     @pl.when(is_worker)
     def _():
@@ -130,9 +156,8 @@
         for half in range(2):
             block[:, half * lane : (half + 1) * lane] = stage[pl.ds(half, COARSE, stride=2), :].astype(BF16)
 
-        @pl.loop(0, COARSE // TILE)
-        def _(step):
-            at = pl.ds(pl.multiple_of(step * TILE, TILE), TILE)
+        for step in range(COARSE // TILE):
+            at = pl.ds(step * TILE, TILE)
             real = dot(big[at, 0:COARSE], block[...])
             imag = dot(big[at, COARSE:], block[...])
             cosine = turn[at, 0:FINE]
@@ -143,9 +168,8 @@
             spec[kind, at, :] = dot(turned, ahead[...])
 
     def back_transform(left, right, conjugate, kind):
-        @pl.loop(0, COARSE // TILE)
-        def _(step):
-            at = pl.ds(pl.multiple_of(step * TILE, TILE), TILE)
+        for step in range(COARSE // TILE):
+            at = pl.ds(step * TILE, TILE)
             left_real = spec[left, at, 0:FINE]
             left_imag = spec[left, at, FINE:]
             right_real = spec[right, at, 0:FINE]
@@ -162,12 +186,11 @@
             cosine = turn[at, 0:FINE]
             sine = turn[at, FINE:]
             mixed[at, :] = (real * cosine + imag * sine).astype(BF16)
-            low = pl.ds(pl.multiple_of(COARSE + step * TILE, TILE), TILE)
+            low = pl.ds(COARSE + step * TILE, TILE)
             mixed[low, :] = (imag * cosine - real * sine).astype(BF16)
 
-        @pl.loop(0, COARSE // TILE)
-        def _(step):
-            at = pl.ds(pl.multiple_of(step * TILE, TILE), TILE)
+        for step in range(COARSE // TILE):
+            at = pl.ds(step * TILE, TILE)
             time = dot(big[at, :], mixed[...]) * (1.0 / total)
             for part in range(2):
                 stage[pl.ds(2 * step * TILE + part, TILE, stride=2), :] = time[
@@ -244,16 +267,18 @@
         drain(back_in, land_sem.at[1])
         drain(corr_in, land_sem.at[2])
 
-    def gather(values, count, result):
+    def gather(values, count, direct, factor, result):
         stage[0 : count * 8, :] = values.reshape(count * 8, lane)
         for piece in range(8):
-            result[:, piece * lane : (piece + 1) * lane] = stage[pl.ds(piece, count, stride=8), :].astype(
-                result.dtype
-            )
-
-    gather(conv_in[...].astype(F32), rows, conv_out)
-    gather(back_in[...].astype(F32), rows, back_out)
-    gather(jnp.sum(corr_in[...].astype(F32), axis=1), 8, corr_out)
+            part = slice(piece * lane, (piece + 1) * lane)
+            value = stage[pl.ds(piece, count, stride=8), :]
+            if direct is not None:
+                value = value + direct[:, part]
+            result[:, part] = value if factor is None else value * factor[:, part].astype(F32)
+
+    gather(conv_in[...].astype(F32), rows, direct_signal, cotangent, conv_out)
+    gather(back_in[...].astype(F32), rows, direct_gated, None, back_out)
+    gather(jnp.sum(corr_in[...].astype(F32), axis=1), 8, None, None, corr_out)
 
     @pl.when(is_worker)
     def _():
@@ -269,13 +294,13 @@
             drain(leave.at[2, 0 : peers - 1], leave_sem.at[2])
 
 
-def exchange(signal, gating, cotangent, filters):
+def exchange(signal, gating, cotangent, filters, skip_weight):
     rows, length = signal.shape
     total = COARSE * FINE
     peers = total // length
-    table_list = tables(total)
+    operands = (signal, gating, cotangent, filters, skip_weight, *tables(total))
     vmem = pl.BlockSpec(memory_space=pltpu.VMEM)
-    hbm = pl.BlockSpec(memory_space=pl.ANY)
+    hbm = pl.BlockSpec(memory_space=pltpu.HBM)
     return pl.pallas_call(
         kernel,
         out_shape=(
@@ -283,9 +308,16 @@
             jax.ShapeDtypeStruct((rows, length), F32),
             jax.ShapeDtypeStruct((8, length), F32),
         ),
-        in_specs=[vmem] * 4 + [hbm] * 4,
+        in_specs=[hbm] * 9,
         out_specs=(vmem, vmem, vmem),
         scratch_shapes=[
+            pltpu.VMEM((rows, length), BF16),
+            pltpu.VMEM((rows, length), BF16),
+            pltpu.VMEM((rows, length), BF16),
+            pltpu.VMEM((rows, length), F32),
+            pltpu.VMEM((rows,), F32),
+            pltpu.VMEM((rows, length), F32),
+            pltpu.VMEM((rows, length), F32),
             pltpu.VMEM((rows, 3, 8, 128), BF16),
             pltpu.VMEM((peers, 3, 8, 128), BF16),
             pltpu.VMEM((peers * 8, 128), F32),
@@ -300,6 +332,7 @@
             pltpu.VMEM((rows, 8, 128), BF16),
             pltpu.VMEM((rows, 8, 128), BF16),
             pltpu.VMEM((8, 4, 8, 128), BF16),
+            pltpu.SemaphoreType.DMA((5,)),
             pltpu.SemaphoreType.DMA((4,)),
             pltpu.SemaphoreType.DMA((4,)),
             pltpu.SemaphoreType.DMA((2,)),
@@ -311,17 +344,14 @@
             collective_id=0, has_side_effects=True, vmem_limit_bytes=40 * 1024 * 1024
         ),
         name="exchange",
-    )(signal, gating, cotangent, filters, *table_list)
+    )(*[pltpu.with_memory_space_constraint(each, pltpu.HBM) for each in operands])
 
 
 def per_device(signal, gating, cotangent, filters, skip_weight):
-    rows, length = signal.shape
-    conv, back, corr = exchange(signal, gating, cotangent, filters)
-    weight = skip_weight[:, None]
-    cot = cotangent.astype(F32)
-    gated = (cot * gating.astype(F32)).astype(BF16).astype(F32)
-    grad_gating = (cot * (conv + weight * signal.astype(F32))).astype(BF16)
-    grad_signal = (back + weight * gated).astype(BF16)
+    rows = signal.shape[0]
+    conv, back, corr = exchange(signal, gating, cotangent, filters, skip_weight)
+    grad_gating = conv.astype(BF16)
+    grad_signal = back.astype(BF16)
     group = lax.axis_size("chan") * rows // filters.shape[0]
     grad_filters = corr * (1.0 / math.sqrt(COARSE * FINE * group))
     return (grad_signal, grad_gating, grad_filters)

time: 62.1 us -> 50.3 us (0.81)
  local copies, waits for them, and re-layouts: 8.6 us -> 0 us
  Pallas kernels: 51 us -> 47.6 us
    unnamed x18 -> x0, local copies, waits for them, and re-layouts: 8.6 us -> none
    pallas_call x1, Pallas kernels: 51 us -> 47.6 us  [exchange(): pl.pallas_call(kernel, out_shape=(jax.ShapeDtypeStruct((rows, length), F3...]
    convert_element_type x1 -> x2, other arithmetic: 0.75 us -> 1.27 us  [the longest x1 0.64 us: per_device(): grad_signal = back.astype(BF16)]
where the time goes in v1:
time: 50.3 us; the launch traced here: 50.1 us
  Pallas kernels  47.6 us (95%)
  other arithmetic  1.89 us (4%)
  between operations  0.64 us (1%)
    pallas_call x1, Pallas kernels, exchange(): pl.pallas_call(kernel, out_shape=(jax.ShapeDtypeStruct((rows, length), F3...  47.6 us

profile of v1, /device:TPU:1, one launch (start us, length us, event | category | flops | bytes accessed | tf_op | source)
XLA Modules:
  0.0 50.1 jit_solution(17853202595660412774)
XLA Ops:
  0.6 47.6 %exchange.1 = (f32[32,1024]{1,0:T(8,128)S(1)}, f32[32,1024]{1,0:T(8,128)S(1)}, f32[8,1024]{1,0:T(8,128)S(1)}) custom-call(bf16[32,1024]{1,0:T(8,128)(2,1)} %signal_hbm.1, bf16[32,1024]{1,0:T(8,128)(2,1)} %gating_hbm.1, bf16[32,1024]{1,0:T(8,128)(2,1)} %cotangent_hbm.1, f32[32,1024]{1,0:T(8,128)} %filters_hbm.1, f32[32]{0:T(128)} %weight_hbm.1, ...), custom_call_target="tpu_custom_call" | custom-call | tf_op jit(solution)/shard_map/exchange/pallas_call | solution.py:304
  48.2 0.6 %convert_element_type.18 = bf16[32,1024]{1,0:T(8,128)(2,1)} convert(f32[32,1024]{1,0:T(8,128)S(1)} %get-tuple-element.6) | non-fusion elementwise | flops 32768 | bytes 196608 | tf_op jit(solution)/shard_map/convert_element_type | solution.py:354
  48.9 0.6 %broadcast_multiply_fusion = f32[8,1024]{1,0:T(8,128)} fusion(f32[8,1024]{1,0:T(8,128)S(1)} %get-tuple-element.8), kind=kLoop, calls=%fused_computation | loop fusion | flops 8192 | bytes 65536 | tf_op jit(solution)/shard_map/mul | solution.py:356
  49.5 0.6 %convert_element_type.19 = bf16[32,1024]{1,0:T(8,128)(2,1)} convert(f32[32,1024]{1,0:T(8,128)S(1)} %get-tuple-element.7) | non-fusion elementwise | flops 32768 | bytes 196608 | tf_op jit(solution)/shard_map/convert_element_type | solution.py:353

commit v2 on v1

--- a/solution.py
+++ b/solution.py
@@ -38,8 +38,8 @@
 
 def kernel(
     signal_hbm, gating_hbm, cotangent_hbm, filters_hbm, weight_hbm, big_hbm, turn_hbm, ahead_hbm, back_hbm,
-    conv_out, back_out, corr_out,
-    signal, gating, cotangent, filters, weight, direct_signal, direct_gated, send, got, stage, big, turn, ahead, back, block, spec, mixed, leave, conv_in, back_in, corr_in,
+    conv_in, back_in, corr_in, direct_signal, direct_gated, cotangent,
+    signal, gating, filters, weight, send, got, stage, big, turn, ahead, back, block, spec, mixed, leave,
     load_sem, table_sem, own_sem, send_sem, got_sem, leave_sem, land_sem,
 ):
     place = lax.axis_index("ctx")
@@ -48,9 +48,12 @@
     peers = 128
     lane = 128
     total = COARSE * FINE
-    worker_low = 1 + chan % 2
     column = place // 4
-    is_worker = place % 4 == worker_low
+
+    def worker_of(filt, channel):
+        return 4 * filt + (1 + channel % 2 + 2 * ((filt + filt // 8) % 2)) % 4
+
+    is_worker = place == worker_of(column, chan)
     home = column // 8
     foreign = home != chan
 
@@ -94,7 +97,7 @@
         filt = 8 * chan + step
         for hop in range(1, 4):
             other = (chan + hop) % 4
-            greet(4 * filt + 1 + other % 2, other)
+            greet(worker_of(filt, other), other)
 
     def spread(values, kind):
         for piece in range(8):
@@ -138,7 +141,7 @@
         @pl.loop(0, rows)
         def _(step):
             filt = (column + step) % rows
-            target = 4 * filt + worker_low
+            target = worker_of(filt, chan)
 
             @pl.when(target != place)
             def _():
@@ -147,6 +150,9 @@
                     send_sem.at[index], got_sem.at[index],
                     device_id=(target, chan), device_id_type=MESH,
                 ).start()
+
+    def turn_to(step):
+        return (place + step) % peers
 
     def drain(ref, sem):
         pltpu.make_async_copy(ref, ref, sem).wait()
@@ -202,7 +208,7 @@
     def scatter(kind, landing):
         @pl.loop(1, peers)
         def _(step):
-            target = (place + step) % peers
+            target = turn_to(step)
             pltpu.make_async_remote_copy(
                 leave.at[kind, target], landing.at[column],
                 leave_sem.at[kind], land_sem.at[kind],
@@ -224,13 +230,11 @@
         scatter(0, conv_in)
         drain(got.at[0 : peers - 1, 2:3], got_sem.at[1])
         ahead_transform(2)
-        back_transform(1, 2, True, 1)
-        scatter(1, back_in)
         back_transform(0, 2, True, 2)
 
         @pl.loop(0, peers)
         def _(step):
-            target = (place + step) % peers
+            target = turn_to(step)
 
             @pl.when(jnp.logical_or(foreign, step > 0))
             def _():
@@ -244,6 +248,9 @@
         def _():
             pltpu.make_async_copy(leave.at[2, place], corr_in.at[column % 8, chan], own_sem.at[3]).start()
 
+        back_transform(1, 2, True, 1)
+        scatter(1, back_in)
+
         drain(send.at[0 : rows - 1, 0:2], send_sem.at[0])
         drain(send.at[0 : rows - 1, 2:3], send_sem.at[1])
         for kind, landing in ((0, conv_in), (1, back_in)):
@@ -267,19 +274,6 @@
         drain(back_in, land_sem.at[1])
         drain(corr_in, land_sem.at[2])
 
-    def gather(values, count, direct, factor, result):
-        stage[0 : count * 8, :] = values.reshape(count * 8, lane)
-        for piece in range(8):
-            part = slice(piece * lane, (piece + 1) * lane)
-            value = stage[pl.ds(piece, count, stride=8), :]
-            if direct is not None:
-                value = value + direct[:, part]
-            result[:, part] = value if factor is None else value * factor[:, part].astype(F32)
-
-    gather(conv_in[...].astype(F32), rows, direct_signal, cotangent, conv_out)
-    gather(back_in[...].astype(F32), rows, direct_gated, None, back_out)
-    gather(jnp.sum(corr_in[...].astype(F32), axis=1), 8, None, None, corr_out)
-
     @pl.when(is_worker)
     def _():
         drain(leave.at[0, 0 : peers - 1], leave_sem.at[0])
@@ -292,6 +286,31 @@
         @pl.when(jnp.logical_not(foreign))
         def _():
             drain(leave.at[2, 0 : peers - 1], leave_sem.at[2])
+
+
+def finish(conv_in, back_in, corr_in, direct_signal, direct_gated, cotangent, *rest):
+    *results, gating_part, signal_part, filter_part, stage, sem = rest
+    parts = (gating_part, signal_part, filter_part)
+    lane = 128
+    scale = 1.0 / math.sqrt(COARSE * FINE * corr_in.shape[1])
+
+    def gather(values, index, last):
+        part = parts[index]
+        count = part.shape[0]
+        stage[index, 0 : count * 8, :] = values.reshape(count * 8, lane)
+        for piece in range(8):
+            at = slice(piece * lane, (piece + 1) * lane)
+            part[:, at] = last(stage[index, pl.ds(piece, count, stride=8), :], at).astype(part.dtype)
+        pltpu.make_async_copy(part, results[index], sem.at[index]).start()
+
+    gather(
+        conv_in[...].astype(F32), 0,
+        lambda value, at: cotangent[:, at].astype(F32) * (value + direct_signal[:, at]),
+    )
+    gather(back_in[...].astype(F32), 1, lambda value, at: value + direct_gated[:, at])
+    gather(jnp.sum(corr_in[...].astype(F32), axis=1), 2, lambda value, at: value * scale)
+    for index in range(3):
+        pltpu.make_async_copy(parts[index], results[index], sem.at[index]).wait()
 
 
 def exchange(signal, gating, cotangent, filters, skip_weight):
@@ -304,20 +323,20 @@
     return pl.pallas_call(
         kernel,
         out_shape=(
+            jax.ShapeDtypeStruct((rows, 8, 128), BF16),
+            jax.ShapeDtypeStruct((rows, 8, 128), BF16),
+            jax.ShapeDtypeStruct((8, 4, 8, 128), BF16),
             jax.ShapeDtypeStruct((rows, length), F32),
             jax.ShapeDtypeStruct((rows, length), F32),
-            jax.ShapeDtypeStruct((8, length), F32),
+            jax.ShapeDtypeStruct((rows, length), BF16),
         ),
         in_specs=[hbm] * 9,
-        out_specs=(vmem, vmem, vmem),
+        out_specs=(vmem,) * 6,
         scratch_shapes=[
-            pltpu.VMEM((rows, length), BF16),
             pltpu.VMEM((rows, length), BF16),
             pltpu.VMEM((rows, length), BF16),
             pltpu.VMEM((rows, length), F32),
             pltpu.VMEM((rows,), F32),
-            pltpu.VMEM((rows, length), F32),
-            pltpu.VMEM((rows, length), F32),
             pltpu.VMEM((rows, 3, 8, 128), BF16),
             pltpu.VMEM((peers, 3, 8, 128), BF16),
             pltpu.VMEM((peers * 8, 128), F32),
@@ -329,9 +348,6 @@
             pltpu.VMEM((3, COARSE, 2 * FINE), F32),
             pltpu.VMEM((2 * COARSE, FINE), BF16),
             pltpu.VMEM((3, peers, 8, 128), BF16),
-            pltpu.VMEM((rows, 8, 128), BF16),
-            pltpu.VMEM((rows, 8, 128), BF16),
-            pltpu.VMEM((8, 4, 8, 128), BF16),
             pltpu.SemaphoreType.DMA((5,)),
             pltpu.SemaphoreType.DMA((4,)),
             pltpu.SemaphoreType.DMA((4,)),
@@ -348,12 +364,28 @@
 
 
 def per_device(signal, gating, cotangent, filters, skip_weight):
-    rows = signal.shape[0]
-    conv, back, corr = exchange(signal, gating, cotangent, filters, skip_weight)
-    grad_gating = conv.astype(BF16)
-    grad_signal = back.astype(BF16)
-    group = lax.axis_size("chan") * rows // filters.shape[0]
-    grad_filters = corr * (1.0 / math.sqrt(COARSE * FINE * group))
+    rows, length = signal.shape
+    landed = exchange(signal, gating, cotangent, filters, skip_weight)
+    vmem = pl.BlockSpec(memory_space=pltpu.VMEM)
+    grad_gating, grad_signal, grad_filters = pl.pallas_call(
+        finish,
+        out_shape=(
+            jax.ShapeDtypeStruct((rows, length), BF16),
+            jax.ShapeDtypeStruct((rows, length), BF16),
+            jax.ShapeDtypeStruct((8, length), F32),
+        ),
+        in_specs=[vmem] * 6,
+        out_specs=(pl.BlockSpec(memory_space=pl.ANY),) * 3,
+        scratch_shapes=[
+            pltpu.VMEM((rows, length), BF16),
+            pltpu.VMEM((rows, length), BF16),
+            pltpu.VMEM((8, length), F32),
+            pltpu.VMEM((3, rows * 8, 128), F32),
+            pltpu.SemaphoreType.DMA((3,)),
+        ],
+        compiler_params=pltpu.CompilerParams(vmem_limit_bytes=16 * 1024 * 1024),
+        name="finish",
+    )(*landed)
     return (grad_signal, grad_gating, grad_filters)
 
 

time: 50.3 us -> 44.3 us (0.88)
  Pallas kernels: 47.6 us -> 43.2 us
  other arithmetic: 1.89 us -> 0 us
    pallas_call x1 -> x2, Pallas kernels: 47.6 us -> 43.2 us  [the longest x1 42.4 us: exchange(): pl.pallas_call(kernel, out_shape=(jax.ShapeDtypeStruct((rows, 8, 128), BF...]
    convert_element_type x2 -> x0, other arithmetic: 1.27 us -> none  [the longest x1 0.64 us: per_device(): grad_signal = back.astype(BF16)]
    mul x1 -> x0, other arithmetic: 0.62 us -> none  [per_device(): grad_filters = corr * (1.0 / math.sqrt(COARSE * FINE * group))]
where the time goes in v2:
time: 44.3 us; the launch traced here: 43.8 us
  Pallas kernels  43.2 us (98%)
  between operations  0.64 us (1%)
    pallas_call x1, Pallas kernels, exchange(): pl.pallas_call(kernel, out_shape=(jax.ShapeDtypeStruct((rows, 8, 128), BF...  42.4 us

profile of v2, /device:TPU:1, one launch (start us, length us, event | category | flops | bytes accessed | tf_op | source)
XLA Modules:
  0.0 43.8 jit_solution(12260253218216614682)
XLA Ops:
  0.6 42.4 %exchange.1 = (bf16[32,8,128]{2,1,0:T(8,128)(2,1)S(1)}, bf16[32,8,128]{2,1,0:T(8,128)(2,1)S(1)}, bf16[8,4,8,128]{3,2,1,0:T(8,128)(2,1)S(1)}, f32[32,1024]{1,0:T(...) custom-call(bf16[32,1024]{1,0:T(8,128)(2,1)} %signal_hbm.1, bf16[32,1024]{1,0:T(8,128)(2,1)} %gating_hbm.1, ...), custom_call_target="tpu_custom_call" | custom-call | tf_op jit(solution)/shard_map/exchange/pallas_call | solution.py:323
  43.1 0.7 %finish.1 = (bf16[32,1024]{1,0:T(8,128)(2,1)}, bf16[32,1024]{1,0:T(8,128)(2,1)}, f32[8,1024]{1,0:T(8,128)}) custom-call(bf16[32,8,128]{2,1,0:T(8,128)(2,1)S(1)} %get-tuple-element.12.conv_in, bf16[32,8,128]{2,1,0:T(8,128)(2,1)S(1)} %get-tuple-element.13.back_in, bf16[8,4,8,128]{3,2,1,0:T(8,128)(2,1)S(1)} %get-tuple-element.14.corr_in, ...), custom_call_target="tpu_custom_call" | custom-call | tf_op jit(solution)/shard_map/finish/pallas_call | solution.py:370

commit v3 on v2

--- a/solution.py
+++ b/solution.py
@@ -12,6 +12,8 @@
 F32 = jnp.float32
 BF16 = jnp.bfloat16
 COARSE = 512
+FAR_RING = (4, 3, 5, 2, 6, 1, 7, 0)
+FAR_ROW = (2, 1, 3, 0)
 FINE = 256
 TILE = 256
 
@@ -49,11 +51,17 @@
     lane = 128
     total = COARSE * FINE
     column = place // 4
-
-    def worker_of(filt, channel):
-        return 4 * filt + (1 + channel % 2 + 2 * ((filt + filt // 8) % 2)) % 4
-
-    is_worker = place == worker_of(column, chan)
+    row, ring, line = place // 32, column % 8, place % 4
+    rows_at = [32 * lax.rem(row + step, 4) for step in range(4)]
+    rings_at = [4 * lax.rem(ring + step, 8) for step in range(8)]
+    lines_at = [lax.rem(line + step, 4) for step in range(4)]
+
+    def worker_line(parity, channel):
+        return lax.rem(1 + channel % 2 + 2 * parity, 4)
+
+    own_parity = lax.rem(row + ring, 2)
+    workers_at = [worker_line(lax.rem(own_parity + step, 2), chan) for step in range(2)]
+    is_worker = line == workers_at[0]
     home = column // 8
     foreign = home != chan
 
@@ -88,16 +96,17 @@
         for copy in table_copies:
             copy.start()
 
-        @pl.loop(1, peers)
-        def _(step):
-            greet((place + step) % peers, chan)
-
-    @pl.loop(0, 8)
-    def _(step):
-        filt = 8 * chan + step
-        for hop in range(1, 4):
-            other = (chan + hop) % 4
-            greet(worker_of(filt, other), other)
+        for ring_at in FAR_RING:
+            for row_at in FAR_ROW:
+                for line_at in range(4):
+                    if ring_at or row_at or line_at:
+                        greet(rows_at[row_at] + rings_at[ring_at] + lines_at[line_at], chan)
+
+    for hop in range(1, 4):
+        other = lax.rem(chan + hop, 4)
+        others_at = [worker_line(lax.rem(chan + ring + step, 2), other) for step in range(2)]
+        for ring_at in FAR_RING:
+            greet(32 * chan + rings_at[ring_at] + others_at[ring_at % 2], other)
 
     def spread(values, kind):
         for piece in range(8):
@@ -135,24 +144,22 @@
     def _():
         pl.semaphore_wait(barrier, 32)
 
-    parts = ((0, 2), (2, 3))
-    for index, (low, high) in enumerate(parts):
-
-        @pl.loop(0, rows)
-        def _(step):
-            filt = (column + step) % rows
-            target = worker_of(filt, chan)
-
-            @pl.when(target != place)
-            def _():
-                pltpu.make_async_remote_copy(
-                    send.at[filt, low:high], got.at[place, low:high],
-                    send_sem.at[index], got_sem.at[index],
-                    device_id=(target, chan), device_id_type=MESH,
-                ).start()
-
-    def turn_to(step):
-        return (place + step) % peers
+    def post(index, low, high, filt, target):
+        pltpu.make_async_remote_copy(
+            send.at[filt, low:high], got.at[place, low:high], send_sem.at[index], got_sem.at[index],
+            device_id=(target, chan), device_id_type=MESH,
+        ).start()
+
+    for index, low, high in ((0, 0, 2), (1, 2, 3)):
+        for ring_at in FAR_RING:
+            for row_at in FAR_ROW:
+                base = rows_at[row_at] + rings_at[ring_at]
+                filt = base // 4
+                target = base + workers_at[(row_at + ring_at) % 2]
+                if ring_at or row_at:
+                    post(index, low, high, filt, target)
+                else:
+                    pl.when(jnp.logical_not(is_worker))(lambda: post(index, low, high, filt, target))
 
     def drain(ref, sem):
         pltpu.make_async_copy(ref, ref, sem).wait()
@@ -205,16 +212,27 @@
 
         leave[kind] = stage[...].reshape(peers, 8, lane).astype(BF16)
 
+    def fan(one, with_self):
+        @pl.loop(0, 8)
+        def _(step):
+            ring_at = 4 * lax.rem(ring + step, 8)
+            for row_at in range(4):
+                for line_at in range(4):
+                    target = rows_at[row_at] + ring_at + lines_at[line_at]
+                    if row_at or line_at:
+                        one(target)
+                    else:
+                        pl.when(jnp.logical_or(step > 0, with_self))(lambda: one(target))
+
     def scatter(kind, landing):
-        @pl.loop(1, peers)
-        def _(step):
-            target = turn_to(step)
+        def one(target):
             pltpu.make_async_remote_copy(
                 leave.at[kind, target], landing.at[column],
                 leave_sem.at[kind], land_sem.at[kind],
                 device_id=(target, chan), device_id_type=MESH,
             ).start()
 
+        fan(one, False)
         pltpu.make_async_copy(leave.at[kind, place], landing.at[column], own_sem.at[1 + kind]).start()
 
     @pl.when(is_worker)
@@ -232,17 +250,14 @@
         ahead_transform(2)
         back_transform(0, 2, True, 2)
 
-        @pl.loop(0, peers)
-        def _(step):
-            target = turn_to(step)
-
-            @pl.when(jnp.logical_or(foreign, step > 0))
-            def _():
-                pltpu.make_async_remote_copy(
-                    leave.at[2, target], corr_in.at[column % 8, chan],
-                    leave_sem.at[2], land_sem.at[2],
-                    device_id=(target, home), device_id_type=MESH,
-                ).start()
+        def send_home(target):
+            pltpu.make_async_remote_copy(
+                leave.at[2, target], corr_in.at[column % 8, chan],
+                leave_sem.at[2], land_sem.at[2],
+                device_id=(target, home), device_id_type=MESH,
+            ).start()
+
+        fan(send_home, foreign)
 
         @pl.when(jnp.logical_not(foreign))
         def _():

time: 44.3 us -> 41.4 us (0.935)
  the two profiles are of different devices: /device:TPU:1 before, /device:TPU:6 now
where the time goes in v3:
time: 41.4 us; the launch traced here: 41.3 us
  Pallas kernels  40.6 us (98%)
  between operations  0.64 us (2%)
    pallas_call x1, Pallas kernels, exchange(): pl.pallas_call(kernel, out_shape=(jax.ShapeDtypeStruct((rows, 8, 128), BF...  39.9 us

profile of v3, /device:TPU:6, one launch (start us, length us, event | category | flops | bytes accessed | tf_op | source)
XLA Modules:
  0.0 41.3 jit_solution(5339072157258613275)
XLA Ops:
  0.6 39.9 %exchange.1 = (bf16[32,8,128]{2,1,0:T(8,128)(2,1)S(1)}, bf16[32,8,128]{2,1,0:T(8,128)(2,1)S(1)}, bf16[8,4,8,128]{3,2,1,0:T(8,128)(2,1)S(1)}, f32[32,1024]{1,0:T(...) custom-call(bf16[32,1024]{1,0:T(8,128)(2,1)} %signal_hbm.1, bf16[32,1024]{1,0:T(8,128)(2,1)} %gating_hbm.1, ...), custom_call_target="tpu_custom_call" | custom-call | tf_op jit(solution)/shard_map/exchange/pallas_call | solution.py:338
  40.5 0.7 %finish.1 = (bf16[32,1024]{1,0:T(8,128)(2,1)}, bf16[32,1024]{1,0:T(8,128)(2,1)}, f32[8,1024]{1,0:T(8,128)}) custom-call(bf16[32,8,128]{2,1,0:T(8,128)(2,1)S(1)} %get-tuple-element.12.conv_in, bf16[32,8,128]{2,1,0:T(8,128)(2,1)S(1)} %get-tuple-element.13.back_in, bf16[8,4,8,128]{3,2,1,0:T(8,128)(2,1)S(1)} %get-tuple-element.14.corr_in, ...), custom_call_target="tpu_custom_call" | custom-call | tf_op jit(solution)/shard_map/finish/pallas_call | solution.py:385

commit v4 on v3

--- a/solution.py
+++ b/solution.py
@@ -57,7 +57,7 @@
     lines_at = [lax.rem(line + step, 4) for step in range(4)]
 
     def worker_line(parity, channel):
-        return lax.rem(1 + channel % 2 + 2 * parity, 4)
+        return 3 * lax.rem(channel, 2) + (1 - 2 * lax.rem(channel, 2)) * (1 - parity)
 
     own_parity = lax.rem(row + ring, 2)
     workers_at = [worker_line(lax.rem(own_parity + step, 2), chan) for step in range(2)]
@@ -213,16 +213,14 @@
         leave[kind] = stage[...].reshape(peers, 8, lane).astype(BF16)
 
     def fan(one, with_self):
-        @pl.loop(0, 8)
-        def _(step):
-            ring_at = 4 * lax.rem(ring + step, 8)
-            for row_at in range(4):
+        for row_at in FAR_ROW:
+            for ring_at in FAR_RING:
                 for line_at in range(4):
-                    target = rows_at[row_at] + ring_at + lines_at[line_at]
-                    if row_at or line_at:
+                    target = rows_at[row_at] + rings_at[ring_at] + lines_at[line_at]
+                    if ring_at or line_at or row_at:
                         one(target)
                     else:
-                        pl.when(jnp.logical_or(step > 0, with_self))(lambda: one(target))
+                        pl.when(with_self)(lambda: one(target))
 
     def scatter(kind, landing):
         def one(target):

time: 41.4 us -> 40.7 us (0.983)
  the two profiles are of different devices: /device:TPU:6 before, /device:TPU:1 now
where the time goes in v4:
time: 40.7 us; the launch traced here: 40.6 us
  Pallas kernels  39.9 us (98%)
  between operations  0.64 us (2%)
    pallas_call x1, Pallas kernels, exchange(): pl.pallas_call(kernel, out_shape=(jax.ShapeDtypeStruct((rows, 8, 128), BF...  39.2 us

profile of v4, /device:TPU:1, one launch (start us, length us, event | category | flops | bytes accessed | tf_op | source)
XLA Modules:
  0.0 40.6 jit_solution(5142145351126518927)
XLA Ops:
  0.6 39.2 %exchange.1 = (bf16[32,8,128]{2,1,0:T(8,128)(2,1)S(1)}, bf16[32,8,128]{2,1,0:T(8,128)(2,1)S(1)}, bf16[8,4,8,128]{3,2,1,0:T(8,128)(2,1)S(1)}, f32[32,1024]{1,0:T(...) custom-call(bf16[32,1024]{1,0:T(8,128)(2,1)} %signal_hbm.1, bf16[32,1024]{1,0:T(8,128)(2,1)} %gating_hbm.1, ...), custom_call_target="tpu_custom_call" | custom-call | tf_op jit(solution)/shard_map/exchange/pallas_call | solution.py:336
  39.8 0.7 %finish.1 = (bf16[32,1024]{1,0:T(8,128)(2,1)}, bf16[32,1024]{1,0:T(8,128)(2,1)}, f32[8,1024]{1,0:T(8,128)}) custom-call(bf16[32,8,128]{2,1,0:T(8,128)(2,1)S(1)} %get-tuple-element.12.conv_in, bf16[32,8,128]{2,1,0:T(8,128)(2,1)S(1)} %get-tuple-element.13.back_in, bf16[8,4,8,128]{3,2,1,0:T(8,128)(2,1)S(1)} %get-tuple-element.14.corr_in, ...), custom_call_target="tpu_custom_call" | custom-call | tf_op jit(solution)/shard_map/finish/pallas_call | solution.py:383

commit v5 on v4

--- a/solution.py
+++ b/solution.py
@@ -180,7 +180,7 @@
             ).astype(BF16)
             spec[kind, at, :] = dot(turned, ahead[...])
 
-    def back_transform(left, right, conjugate, kind):
+    def back_transform(left, right, conjugate, kind, after=None):
         for step in range(COARSE // TILE):
             at = pl.ds(step * TILE, TILE)
             left_real = spec[left, at, 0:FINE]
@@ -210,7 +210,15 @@
                     :, part * lane : (part + 1) * lane
                 ]
 
-        leave[kind] = stage[...].reshape(peers, 8, lane).astype(BF16)
+            if after is not None:
+                half = peers * TILE // COARSE
+                leave[kind, step * half : (step + 1) * half] = (
+                    stage[2 * step * TILE : 2 * (step + 1) * TILE, :].reshape(half, 8, lane).astype(BF16)
+                )
+                after(step)
+
+        if after is None:
+            leave[kind] = stage[...].reshape(peers, 8, lane).astype(BF16)
 
     def fan(one, with_self):
         for row_at in FAR_ROW:
@@ -261,8 +269,25 @@
         def _():
             pltpu.make_async_copy(leave.at[2, place], corr_in.at[column % 8, chan], own_sem.at[3]).start()
 
-        back_transform(1, 2, True, 1)
-        scatter(1, back_in)
+        def send_half(step):
+            for ring_at in FAR_RING:
+                for row_at in (2 * step, 2 * step + 1):
+                    for line_at in range(4):
+                        target = 32 * row_at + rings_at[ring_at] + lines_at[line_at]
+                        if ring_at or line_at:
+                            send_back(target)
+                        else:
+                            pl.when(row != row_at)(lambda: send_back(target))
+
+        def send_back(target):
+            pltpu.make_async_remote_copy(
+                leave.at[1, target], back_in.at[column],
+                leave_sem.at[1], land_sem.at[1],
+                device_id=(target, chan), device_id_type=MESH,
+            ).start()
+
+        back_transform(1, 2, True, 1, send_half)
+        pltpu.make_async_copy(leave.at[1, place], back_in.at[column], own_sem.at[2]).start()
 
         drain(send.at[0 : rows - 1, 0:2], send_sem.at[0])
         drain(send.at[0 : rows - 1, 2:3], send_sem.at[1])

time: 40.7 us -> 39.7 us (0.975)
  Pallas kernels: 39.9 us -> 38.7 us
    pallas_call x1, Pallas kernels: 39.2 us -> 38 us  [exchange(): pl.pallas_call(kernel, out_shape=(jax.ShapeDtypeStruct((rows, 8, 128), BF...]
where the time goes in v5:
time: 39.7 us; the launch traced here: 39.4 us
  Pallas kernels  38.7 us (97%)
  between operations  0.64 us (2%)
    pallas_call x1, Pallas kernels, exchange(): pl.pallas_call(kernel, out_shape=(jax.ShapeDtypeStruct((rows, 8, 128), BF...  38 us

profile of v5, /device:TPU:1, one launch (start us, length us, event | category | flops | bytes accessed | tf_op | source)
XLA Modules:
  0.0 39.4 jit_solution(11915823563284717202)
XLA Ops:
  0.6 38.0 %exchange.1 = (bf16[32,8,128]{2,1,0:T(8,128)(2,1)S(1)}, bf16[32,8,128]{2,1,0:T(8,128)(2,1)S(1)}, bf16[8,4,8,128]{3,2,1,0:T(8,128)(2,1)S(1)}, f32[32,1024]{1,0:T(...) custom-call(bf16[32,1024]{1,0:T(8,128)(2,1)} %signal_hbm.1, bf16[32,1024]{1,0:T(8,128)(2,1)} %gating_hbm.1, ...), custom_call_target="tpu_custom_call" | custom-call | tf_op jit(solution)/shard_map/exchange/pallas_call | solution.py:361
  38.6 0.7 %finish.1 = (bf16[32,1024]{1,0:T(8,128)(2,1)}, bf16[32,1024]{1,0:T(8,128)(2,1)}, f32[8,1024]{1,0:T(8,128)}) custom-call(bf16[32,8,128]{2,1,0:T(8,128)(2,1)S(1)} %get-tuple-element.12.conv_in, bf16[32,8,128]{2,1,0:T(8,128)(2,1)S(1)} %get-tuple-element.13.back_in, bf16[8,4,8,128]{3,2,1,0:T(8,128)(2,1)S(1)} %get-tuple-element.14.corr_in, ...), custom_call_target="tpu_custom_call" | custom-call | tf_op jit(solution)/shard_map/finish/pallas_call | solution.py:408

commit v6 on v5

--- a/solution.py
+++ b/solution.py
@@ -254,7 +254,18 @@
         scatter(0, conv_in)
         drain(got.at[0 : peers - 1, 2:3], got_sem.at[1])
         ahead_transform(2)
-        back_transform(0, 2, True, 2)
+        def halves(one, with_self):
+            def send_half(step):
+                for ring_at in FAR_RING:
+                    for row_at in (2 * step, 2 * step + 1):
+                        for line_at in range(4):
+                            target = 32 * row_at + rings_at[ring_at] + lines_at[line_at]
+                            if ring_at or line_at:
+                                one(target)
+                            else:
+                                pl.when(jnp.logical_or(row != row_at, with_self))(lambda: one(target))
+
+            return send_half
 
         def send_home(target):
             pltpu.make_async_remote_copy(
@@ -263,21 +274,11 @@
                 device_id=(target, home), device_id_type=MESH,
             ).start()
 
-        fan(send_home, foreign)
+        back_transform(0, 2, True, 2, halves(send_home, foreign))
 
         @pl.when(jnp.logical_not(foreign))
         def _():
             pltpu.make_async_copy(leave.at[2, place], corr_in.at[column % 8, chan], own_sem.at[3]).start()
-
-        def send_half(step):
-            for ring_at in FAR_RING:
-                for row_at in (2 * step, 2 * step + 1):
-                    for line_at in range(4):
-                        target = 32 * row_at + rings_at[ring_at] + lines_at[line_at]
-                        if ring_at or line_at:
-                            send_back(target)
-                        else:
-                            pl.when(row != row_at)(lambda: send_back(target))
 
         def send_back(target):
             pltpu.make_async_remote_copy(
@@ -286,7 +287,7 @@
                 device_id=(target, chan), device_id_type=MESH,
             ).start()
 
-        back_transform(1, 2, True, 1, send_half)
+        back_transform(1, 2, True, 1, halves(send_back, False))
         pltpu.make_async_copy(leave.at[1, place], back_in.at[column], own_sem.at[2]).start()
 
         drain(send.at[0 : rows - 1, 0:2], send_sem.at[0])

time: 39.7 us -> 39.8 us (level)
  the two profiles are of different devices: /device:TPU:1 before, /device:TPU:56 now
where the time goes in v6:
time: 39.8 us; the launch traced here: 39.6 us
  Pallas kernels  39 us (98%)
  between operations  0.64 us (2%)
    pallas_call x1, Pallas kernels, exchange(): pl.pallas_call(kernel, out_shape=(jax.ShapeDtypeStruct((rows, 8, 128), BF...  38.2 us

profile of v6, /device:TPU:56, one launch (start us, length us, event | category | flops | bytes accessed | tf_op | source)
XLA Modules:
  0.0 39.6 jit_solution(4673181763908241132)
XLA Ops:
  0.6 38.2 %exchange.1 = (bf16[32,8,128]{2,1,0:T(8,128)(2,1)S(1)}, bf16[32,8,128]{2,1,0:T(8,128)(2,1)S(1)}, bf16[8,4,8,128]{3,2,1,0:T(8,128)(2,1)S(1)}, f32[32,1024]{1,0:T(...) custom-call(bf16[32,1024]{1,0:T(8,128)(2,1)} %signal_hbm.1, bf16[32,1024]{1,0:T(8,128)(2,1)} %gating_hbm.1, ...), custom_call_target="tpu_custom_call" | custom-call | tf_op jit(solution)/shard_map/exchange/pallas_call | solution.py:362
  38.9 0.7 %finish.1 = (bf16[32,1024]{1,0:T(8,128)(2,1)}, bf16[32,1024]{1,0:T(8,128)(2,1)}, f32[8,1024]{1,0:T(8,128)}) custom-call(bf16[32,8,128]{2,1,0:T(8,128)(2,1)S(1)} %get-tuple-element.12.conv_in, bf16[32,8,128]{2,1,0:T(8,128)(2,1)S(1)} %get-tuple-element.13.back_in, bf16[8,4,8,128]{3,2,1,0:T(8,128)(2,1)S(1)} %get-tuple-element.14.corr_in, ...), custom_call_target="tpu_custom_call" | custom-call | tf_op jit(solution)/shard_map/finish/pallas_call | solution.py:409
